TPU v7x, 32 devices: a whole 2x2x4 slice. The times are simulated.
32 devices in a mesh: groups: 2 (over y), rows: 4 (over z), mp: 2 (over x), pair: 2 (over core).
Axes of the slice: x: 2, y: 2, z: 4, core: 2. Of those that a mesh axis runs over, the one named last changes fastest.
Arguments:
- query_rows: bfloat16 [2048, 512], P(('groups', 'rows', 'pair'), 'mp'), parts along dimension 0, may hold values from -240 to 240
- key_rows: bfloat16 [65536, 512], P(('groups', 'rows', 'pair'), 'mp'), parts along dimension 0, may hold values from -24 to 24
- value_rows: bfloat16 [65536, 512], P(('groups', 'rows', 'pair'), 'mp'), parts along dimension 0, may hold values from -6 to 6
- cotangent: bfloat16 [2048, 512], P(('groups', 'rows', 'pair'), 'mp'), parts along dimension 0, may hold values from -1536 to 1536
- train_rows: int32 [16], P('groups'), parts along dimension 0, may hold values from 1 to 12288, as said below
- test_rows: int32 [16], P('groups'), parts along dimension 0, may hold values from 32 to 128
- block_table: int32 [128], P('groups'), parts along dimension 0, may hold values from 0 to 7, as said below
Outputs:
- query_grad: bfloat16 [2048, 512], P(('groups', 'rows', 'pair'), 'mp'), parts along dimension 0
- key_grad: bfloat16 [65536, 512], P(('groups', 'rows', 'pair'), 'mp'), parts along dimension 0
- value_grad: bfloat16 [65536, 512], P(('groups', 'rows', 'pair'), 'mp'), parts along dimension 0
There are 2 independent parts, one for each index of `groups`. A program takes and returns all parts, laid end to end along the dimension named above; each array names one. Nothing has to cross between parts.
Inputs may be any that keep to these rules, and one draw needn't show every extreme that they name: block_table names table t exactly ceil(train_rows[t] / 512) times; the largest table has 24 full blocks. `block_table`: every table is named at least once.
All inputs are finite; a program needn't handle non-finite values.
Results may differ from a plain program's by a relative error of at most 0.0075.
Values may be sent and summed in bfloat16 or wider, within the bound.
No kernel may reach another device: no remote copies, remote signals or barrier semaphores. Data moves between devices by JAX's collectives and lax.ppermute only.
A program may use at most 64 MiB of HBM per device.

v0:
```python
import math
import jax
import jax.numpy as jnp
from jax import lax
from jax.sharding import PartitionSpec as P

HD = 64
TEST = 128
BLK = 512
NEG = -1e30


def combined_all(value, axis, join):
    pieces = jax.tree.map(lambda part: lax.all_gather(part, axis), value)
    head = jax.tree.map(lambda part: part[0], pieces)
    tail = jax.tree.map(lambda part: part[1:], pieces)
    total, _ = lax.scan(lambda total, piece: (join(total, piece), None), head, tail)
    return total


def table_lookup(positions, entries):
    matches = positions[:, None] == jnp.arange(entries.shape[0], dtype=jnp.int32)[None, :]
    return jnp.sum(jnp.where(matches, entries[None, :], 0), axis=1)


def merge_two(former, latter):
    new_peak = jnp.maximum(former[0], latter[0])
    return (
        new_peak,
        former[1] * jnp.exp(former[0] - new_peak) + latter[1] * jnp.exp(latter[0] - new_peak),
    )


def contract_rows(left, right):
    return lax.dot_general(
        left, right, (((0,), (0,)), ((), ())), preferred_element_type=jnp.float32
    )


def contract_features(left, right):
    return lax.dot_general(
        left, right, (((1,), (1,)), ((), ())), preferred_element_type=jnp.float32
    )


def local(query_rows, key_rows, value_rows, cotangent, train_rows, test_rows, block_table):
    device = lax.axis_index(("rows", "pair"))
    local_rows = query_rows.shape[0]
    features = query_rows.shape[1]
    head_count = features // HD
    blocks = key_rows.shape[0] // BLK
    tables = train_rows.shape[0]
    query_count = tables * TEST
    stacked = head_count * TEST
    score_scale = 1.0 / math.sqrt(HD)
    row_ids = device * local_rows + jnp.arange(local_rows, dtype=jnp.int32)
    query_live = row_ids % TEST < table_lookup(row_ids // TEST, test_rows)
    live_grads = jnp.where(query_live[:, None], cotangent, jnp.zeros_like(cotangent))
    all_queries, all_grads = (
        lax.all_gather(query_rows, ("rows", "pair"), axis=0, tiled=True),
        lax.all_gather(live_grads, ("rows", "pair"), axis=0, tiled=True),
    )
    head_of_feature = jnp.arange(features, dtype=jnp.int32) // HD
    head_mask = head_of_feature[None, :] == jnp.arange(head_count, dtype=jnp.int32)[:, None]

    def expand(rows):
        shaped = rows.reshape(tables, 1, TEST, features)
        masked = jnp.where(head_mask[None, :, None, :], shaped, jnp.zeros_like(shaped))
        return masked.reshape(tables, stacked, features)

    def collapse(product):
        shaped = product.reshape(head_count, TEST, features)
        return jnp.sum(jnp.where(head_mask[:, None, :], shaped, 0.0), axis=0)

    spread_queries = expand(all_queries)
    spread_grads = expand(all_grads)
    block_ids = jnp.arange(block_table.shape[0], dtype=jnp.int32)
    my_blocks = device * blocks + jnp.arange(blocks, dtype=jnp.int32)
    block_owner = lax.dynamic_slice_in_dim(block_table, device * blocks, blocks)
    earlier = (block_table[None, :] == block_owner[:, None]) & (
        block_ids[None, :] < my_blocks[:, None]
    )
    ordinal = jnp.sum(jnp.where(earlier, 1, 0), axis=1).astype(jnp.int32)
    live_keys = table_lookup(block_owner, train_rows) - ordinal * BLK
    key_blocks = key_rows.reshape(blocks, BLK, features)
    value_blocks = value_rows.reshape(blocks, BLK, features)
    key_index = jnp.arange(BLK, dtype=jnp.int32)
    block_inputs = (block_owner, live_keys, key_blocks, value_blocks)

    def block_scores(which_table, live_count, key_block):
        query_block = spread_queries[which_table]
        raw_scores = contract_features(query_block, key_block) * score_scale
        return (query_block, jnp.where(key_index[None, :] < live_count, raw_scores, NEG))

    def stats_step(running, inputs):
        which_table, live_count, key_block, value_block = inputs
        _, scores = block_scores(which_table, live_count, key_block)
        block_peak = jnp.max(scores, axis=1)
        weights = jnp.exp(scores - block_peak[:, None])
        block_mass = jnp.sum(weights, axis=1)
        old_peak = running[0][which_table]
        old_mass = running[1][which_table]
        new_peak = jnp.maximum(old_peak, block_peak)
        old_weight = jnp.exp(old_peak - new_peak)
        new_weight = jnp.exp(block_peak - new_peak)
        updated = [
            running[0].at[which_table].set(new_peak),
            running[1].at[which_table].set(old_mass * old_weight + block_mass * new_weight),
        ]
        return (tuple(updated), None)

    initial = [
        jnp.full((tables, stacked), NEG, jnp.float32),
        jnp.zeros((tables, stacked), jnp.float32),
    ]
    result, _ = lax.scan(stats_step, tuple(initial), block_inputs)
    peaks, masses = result
    peaks, masses = combined_all((peaks, masses), ("rows", "pair"), merge_two)

    def inner_step(running, inputs):
        which_table, live_count, key_block, value_block = inputs
        _, scores = block_scores(which_table, live_count, key_block)
        dprobs = contract_features(spread_grads[which_table], value_block)
        block_peak = jnp.max(scores, axis=1)
        weights_low = jnp.exp(scores - block_peak[:, None]).astype(jnp.bfloat16).astype(jnp.float32)
        term = (
            jnp.sum(weights_low * dprobs, axis=1)
            * jnp.exp(block_peak - peaks[which_table])
            / masses[which_table]
        )
        return (running.at[which_table].add(term), None)

    inner_terms, _ = lax.scan(inner_step, jnp.zeros((tables, stacked), jnp.float32), block_inputs)
    inner = lax.psum(inner_terms, ("rows", "pair"))

    def grad_step(running, inputs):
        which_table, live_count, key_block, value_block = inputs
        query_block, scores = block_scores(which_table, live_count, key_block)
        grad_block = spread_grads[which_table]
        probs = jnp.exp(scores - peaks[which_table][:, None]) / masses[which_table][:, None]
        dprobs = contract_features(grad_block, value_block)
        probs_low = probs.astype(jnp.bfloat16)
        value_part = contract_rows(probs_low, grad_block)
        dscores = (probs * (dprobs - inner[which_table][:, None])).astype(jnp.bfloat16)
        key_part = contract_rows(dscores, query_block) * score_scale
        query_part = (
            collapse(jnp.dot(dscores, key_block, preferred_element_type=jnp.float32)) * score_scale
        )
        running = running.at[which_table].add(query_part)
        return (running, (key_part.astype(jnp.bfloat16), value_part.astype(jnp.bfloat16)))

    query_terms, (key_parts, value_parts) = lax.scan(
        grad_step, jnp.zeros((tables, TEST, features), jnp.float32), block_inputs
    )
    query_total = lax.psum_scatter(
        query_terms.reshape(query_count, features),
        ("rows", "pair"),
        scatter_dimension=0,
        tiled=True,
    )
    return (
        query_total.astype(jnp.bfloat16),
        key_parts.reshape(blocks * BLK, features),
        value_parts.reshape(blocks * BLK, features),
    )


def solution(mesh):
    in_specs = (
        P(("groups", "rows", "pair"), "mp"),
        P(("groups", "rows", "pair"), "mp"),
        P(("groups", "rows", "pair"), "mp"),
        P(("groups", "rows", "pair"), "mp"),
        P("groups"),
        P("groups"),
        P("groups"),
    )
    out_specs = (
        P(("groups", "rows", "pair"), "mp"),
        P(("groups", "rows", "pair"), "mp"),
        P(("groups", "rows", "pair"), "mp"),
    )
    return jax.shard_map(local, mesh=mesh, in_specs=in_specs, out_specs=out_specs, check_vma=False)
```

profile of v0, /device:TPU:0, one launch (start us, length us, event | category | flops | bytes accessed | tf_op | source)
XLA Modules:
  0.0 357.1 jit_solution(11898617688526695184)
XLA Ops:
  11.4 16.6 %all_gather.23 = bf16[1024,256]{1,0:T(8,128)(2,1)S(1)} all-gather(bf16[128,256]{1,0:T(8,128)(2,1)S(1)} %broadcast_select_fusion.3), channel_id=1, replica_groups=mesh['groups'=2,'rows'=4,'mp'=2,'pair'=2] {'rows','pair'}, dimensions={0}, use_global_device_ids=true | all-gather | bytes 589824 | tf_op jit(solution)/shard_map/all_gather | solution.py:61
  28.0 14.9 %all_gather.18 = bf16[1024,256]{1,0:T(8,128)(2,1)S(1)} all-gather(bf16[128,256]{1,0:T(8,128)(2,1)} %param.23), channel_id=1, replica_groups=mesh['groups'=2,'rows'=4,'mp'=2,'pair'=2] {'rows','pair'}, dimensions={0}, use_global_device_ids=true | all-gather | bytes 589824 | tf_op jit(solution)/shard_map/all_gather | solution.py:60
  42.9 1.7 bitcast_select_fusion
  44.6 55.1 %while.60 = (s32[]{:T(128)}, f32[8,512]{1,0:T(8,128)S(1)}, f32[8,512]{1,0:T(8,128)S(1)}, s32[8]{0:T(128)S(1)}, s32[8]{0:T(128)S(1)}, /*index=5*/bf16[8,512,256]{...) while((s32[]{:T(128)}, f32[8,512]{1,0:T(8,128)S(1)}, ...), condition=%wide.region_7.8_spmd.clone.clone, body=%wide.region_3.7_spmd.clone.sunk.clone | while | flops 135532048 | bytes 2649797 | solution.py:116
  49.2 1.4 fusion.112
  56.0 1.4 fusion.112
  62.9 1.4 fusion.112
  69.8 1.4 fusion.112
  76.7 1.4 fusion.112
  83.6 1.4 fusion.112
  90.5 1.4 fusion.112
  97.4 1.4 fusion.112
  99.8 14.2 %all-gather.1 = f32[64,512]{1,0:T(8,128)S(1)} all-gather(f32[8,512]{1,0:T(8,128)S(1)} %get-tuple-element.259), channel_id=3, replica_groups=mesh['groups'=2,'rows'=4,'mp'=2,'pair'=2] {'rows','pair'}, dimensions={0}, use_global_device_ids=true | all-gather | bytes 147456 | tf_op jit(solution)/shard_map/all_gather | solution.py:14
  114.0 14.0 %all-gather = f32[64,512]{1,0:T(8,128)S(1)} all-gather(f32[8,512]{1,0:T(8,128)S(1)} %get-tuple-element.258), channel_id=2, replica_groups=mesh['groups'=2,'rows'=4,'mp'=2,'pair'=2] {'rows','pair'}, dimensions={0}, use_global_device_ids=true | all-gather | bytes 147456 | tf_op jit(solution)/shard_map/all_gather | solution.py:14
  128.3 61.7 %while.61 = (s32[]{:T(128)}, f32[8,512]{1,0:T(8,128)S(1)}, s32[8]{0:T(128)S(1)}, s32[8]{0:T(128)S(1)}, bf16[8,512,256]{2,1,0:T(8,128)(2,1)}, /*index=5*/bf16[8,5...) while((s32[]{:T(128)}, f32[8,512]{1,0:T(8,128)S(1)}, ...), condition=%wide.region_14.15_spmd.clone.clone, body=%wide.region_10.14_spmd.clone.sunk.clone | while | flops 270534656 | bytes 3170525 | solution.py:133
  132.6 1.4 fusion.115
  134.0 1.3 fusion.116
  140.3 1.4 fusion.115
  141.7 1.3 fusion.116
  148.1 1.4 fusion.115
  149.4 1.3 fusion.116
  155.8 1.4 fusion.115
  163.5 1.4 fusion.115
  164.9 1.3 fusion.116
  171.2 1.4 fusion.115
  172.6 1.3 fusion.116
  178.9 1.4 fusion.115
  186.6 1.4 fusion.115
  190.1 29.2 %psum.7 = f32[8,512]{1,0:T(8,128)S(1)} all-reduce(f32[8,512]{1,0:T(8,128)S(1)} %get-tuple-element.262), channel_id=1, replica_groups=mesh['groups'=2,'rows'=4,'mp'=2,'pair'=2] {'rows','pair'}, use_global_device_ids=true, to_apply=%region_15.16 | all-reduce | flops 4096 | bytes 32768 | tf_op jit(solution)/shard_map/psum | solution.py:134
  219.4 97.7 %while.62 = (s32[]{:T(128)}, f32[8,128,256]{2,1,0:T(8,128)S(1)}, bf16[8,512,256]{2,1,0:T(8,128)(2,1)}, bf16[8,512,256]{2,1,0:T(8,128)(2,1)}, s32[8]{0:T(128)S(1)...) while((s32[]{:T(128)}, f32[8,128,256]{2,1,0:T(8,128)S(1)}, ...), condition=%wide.region_19.20_spmd.clone.clone, body=%wide.region_16.19_spmd.clone.sunk.clone | while | flops 673908224 | bytes 7627025 | solution.py:152
  223.8 1.5 fusion.127
  229.6 2.0 fusion.131
  236.0 1.5 fusion.127
  241.8 2.0 fusion.131
  248.3 1.5 fusion.127
  254.0 2.0 fusion.131
  260.5 1.5 fusion.127
  266.2 2.0 fusion.131
  272.7 1.5 fusion.127
  278.4 2.0 fusion.131
  284.9 1.5 fusion.127
  290.6 2.0 fusion.131
  297.1 1.5 fusion.127
  302.9 2.0 fusion.131
  309.3 1.5 fusion.127
  315.1 2.0 fusion.131
  318.1 30.6 %reduce-scatter.2.cloned.1.call-done = f32[128,256]{1,0:T(8,128)} async-done(((f32[1024,256]{1,0:T(8,128)}), f32[128,256]{1,0:T(8,128)}) %reduce-scatter.2.cloned.1.call-update) | async-done | bytes 131088 | tf_op jit(solution)/shard_map/reduce_scatter | solution.py:155
  348.7 1.5 convert_element_type.21
  (241 shorter events, 118.2 us)
Async XLA Ops:
  7.2 341.5 %reduce-scatter.2.cloned.1.call-start = ((), (), s32[]{:S(2)}) async-start(), calls=%async_computation.1 | async-start | bytes 1179648 | tf_op jit(solution)/shard_map/reduce_scatter | solution.py:155
  42.9 1.7 copy-start.1
  128.3 91.1 %copy-start.2 = (s32[3]{0:T(128)S(1)}, s32[3]{0:T(128)}, u32[]{:S(2)}) copy-start(s32[3]{0:T(128)} %constant.200.clone.2) | copy-start | bytes 40
  317.1 1.0 copy-start
Sparse Core Ops, SparseCore 0:
  318.2 30.4 reduce-scatter.1
where the time goes:
time: 360 us; the launch traced here: 357 us
  matrix products  89.4 us (25%)
  blocking collectives  89 us (25%)
  other arithmetic  55.6 us (15%)
  loops' own time  45.8 us (13%)
  local copies, waits for them, and re-layouts  32.5 us (9%)
  waiting for transfers between devices  30.6 us (8%)
  between operations  14.2 us (4%)
    dot_general x40, matrix products, contract_features(): lax.dot_general(left, right, (((1,), (1,)), ((), ())), preferred_element_...  54.7 us
    reduce_scatter x1, waiting for transfers between devices, local(): lax.psum_scatter(query_terms.reshape(query_count, features), ('rows', 'pa...  30.6 us
    psum x1, blocking collectives, local(): inner = lax.psum(inner_terms, ('rows', 'pair'))  29.2 us
    dynamic_slice x48, local copies, waits for them, and re-layouts, local(): result, _ = lax.scan(stats_step, tuple(initial), block_inputs)  29 us
    all_gather x2, blocking collectives, combined_all(): pieces = jax.tree.map(lambda part: lax.all_gather(part, axis), value)  28.2 us
    another operation x42, other arithmetic  27.8 us
    dot_general x16, matrix products, contract_rows(): lax.dot_general(left, right, (((0,), (0,)), ((), ())), preferred_element_...  24.6 us
    all_gather x1, blocking collectives, local(): lax.all_gather(live_grads, ('rows', 'pair'), axis=0, tiled=True)  16.6 us
  transfers between devices with their start and end apart: 1, of which 1 were waited for; matrix products, arithmetic and copies ran while one was open for 0% of the time, Pallas kernels for 0%

commit v1 on v0

--- a/solution.py
+++ b/solution.py
@@ -8,6 +8,18 @@
 TEST = 128
 BLK = 512
 NEG = -1e30
+
+
+def ring_gather(value, axis, dim):
+    ways, here, hop = (lax.axis_size(axis), lax.axis_index(axis), value.shape[dim])
+    dims = [n * ways if d == dim else n for d, n in enumerate(value.shape)]
+    full = lax.dynamic_update_slice_in_dim(
+        jnp.zeros(dims, value.dtype), value, here * hop, axis=dim
+    )
+    for far in range(1, ways):
+        value = lax.ppermute(value, axis, [(d, (d + 1) % ways) for d in range(ways)])
+        full = lax.dynamic_update_slice_in_dim(full, value, (here - far) % ways * hop, axis=dim)
+    return full
 
 
 def combined_all(value, axis, join):
@@ -57,7 +69,7 @@
     query_live = row_ids % TEST < table_lookup(row_ids // TEST, test_rows)
     live_grads = jnp.where(query_live[:, None], cotangent, jnp.zeros_like(cotangent))
     all_queries, all_grads = (
-        lax.all_gather(query_rows, ("rows", "pair"), axis=0, tiled=True),
+        ring_gather(query_rows, ("rows", "pair"), 0),
         lax.all_gather(live_grads, ("rows", "pair"), axis=0, tiled=True),
     )
     head_of_feature = jnp.arange(features, dtype=jnp.int32) // HD

time: 360 us -> 376 us (1.044)
  waiting for transfers between devices: 30.6 us -> 63.1 us
  blocking collectives: 89 us -> 70.8 us
    ppermute x0 -> x7, waiting for transfers between devices: none -> 32.5 us  [ring_gather(): lax.ppermute(value, axis, [(d, (d + 1) % ways) for d in range(ways)])]
    all_gather x1 -> x0, blocking collectives: 14.9 us -> none  [local(): lax.all_gather(query_rows, ('rows', 'pair'), axis=0, tiled=True)]
  transfers between devices with their start and end apart: 1 -> 8, of which waited for: 1 -> 7; matrix products, arithmetic and copies ran while one was open for 0% -> 1% of each run, Pallas kernels for 0% -> 0%
where the time goes in v1:
time: 376 us; the launch traced here: 373 us
  matrix products  89.4 us (24%)
  blocking collectives  70.8 us (19%)
  waiting for transfers between devices  63.1 us (17%)
  other arithmetic  55.6 us (15%)
  loops' own time  45.8 us (12%)
  local copies, waits for them, and re-layouts  33.5 us (9%)
  between operations  14.2 us (4%)
    dot_general x40, matrix products, contract_features(): lax.dot_general(left, right, (((1,), (1,)), ((), ())), preferred_element_...  54.7 us
    ppermute x7, waiting for transfers between devices, ring_gather(): lax.ppermute(value, axis, [(d, (d + 1) % ways) for d in range(ways)])  32.5 us
    reduce_scatter x1, waiting for transfers between devices, local(): lax.psum_scatter(query_terms.reshape(query_count, features), ('rows', 'pa...  30.6 us
    dynamic_slice x48, local copies, waits for them, and re-layouts, local(): result, _ = lax.scan(stats_step, tuple(initial), block_inputs)  29 us
    all_gather x2, blocking collectives, combined_all(): pieces = jax.tree.map(lambda part: lax.all_gather(part, axis), value)  27.9 us
    another operation x42, other arithmetic  27.8 us
    psum x1, blocking collectives, local(): inner = lax.psum(inner_terms, ('rows', 'pair'))  26.1 us
    dot_general x16, matrix products, contract_rows(): lax.dot_general(left, right, (((0,), (0,)), ((), ())), preferred_element_...  24.6 us
  transfers between devices with their start and end apart: 8, of which 7 were waited for; matrix products, arithmetic and copies ran while one was open for 1% of the time, Pallas kernels for 0%

profile of v1, /device:TPU:0, one launch (start us, length us, event | category | flops | bytes accessed | tf_op | source)
XLA Modules:
  0.0 373.3 jit_solution(6385626040197426120)
XLA Ops:
  11.9 16.7 %all_gather.19 = bf16[1024,256]{1,0:T(8,128)(2,1)S(1)} all-gather(bf16[128,256]{1,0:T(8,128)(2,1)S(1)} %broadcast_select_fusion.3), channel_id=1, replica_groups=mesh['groups'=2,'rows'=4,'mp'=2,'pair'=2] {'rows','pair'}, dimensions={0}, use_global_device_ids=true | all-gather | bytes 589824 | tf_op jit(solution)/shard_map/all_gather | solution.py:73
  29.9 5.1 %collective-permute-done.1 = bf16[128,256]{1,0:T(8,128)(2,1)S(1)} collective-permute-done((bf16[128,256]{1,0:T(8,128)(2,1)S(1)}, bf16[128,256]{1,0:T(8,128)(2,1)S(1)}, u32[]{:S(2)}, u32[]{:S(2)}) %collective-permute-start.1) | collective-permute-done | bytes 65568 | tf_op jit(solution)/shard_map/ppermute | solution.py:20
  35.0 5.5 %collective-permute-done.2 = bf16[128,256]{1,0:T(8,128)(2,1)S(1)} collective-permute-done((bf16[128,256]{1,0:T(8,128)(2,1)S(1)}, bf16[128,256]{1,0:T(8,128)(2,1)S(1)}, u32[]{:S(2)}, u32[]{:S(2)}) %collective-permute-start.2) | collective-permute-done | bytes 65568 | tf_op jit(solution)/shard_map/ppermute | solution.py:20
  40.5 5.5 %collective-permute-done.3 = bf16[128,256]{1,0:T(8,128)(2,1)S(1)} collective-permute-done((bf16[128,256]{1,0:T(8,128)(2,1)S(1)}, bf16[128,256]{1,0:T(8,128)(2,1)S(1)}, u32[]{:S(2)}, u32[]{:S(2)}) %collective-permute-start.3) | collective-permute-done | bytes 65568 | tf_op jit(solution)/shard_map/ppermute | solution.py:20
  46.0 5.5 %collective-permute-done.4 = bf16[128,256]{1,0:T(8,128)(2,1)S(1)} collective-permute-done((bf16[128,256]{1,0:T(8,128)(2,1)S(1)}, bf16[128,256]{1,0:T(8,128)(2,1)S(1)}, u32[]{:S(2)}, u32[]{:S(2)}) %collective-permute-start.4) | collective-permute-done | bytes 65568 | tf_op jit(solution)/shard_map/ppermute | solution.py:20
  51.5 5.5 %collective-permute-done.5 = bf16[128,256]{1,0:T(8,128)(2,1)S(1)} collective-permute-done((bf16[128,256]{1,0:T(8,128)(2,1)S(1)}, bf16[128,256]{1,0:T(8,128)(2,1)S(1)}, u32[]{:S(2)}, u32[]{:S(2)}) %collective-permute-start.5) | collective-permute-done | bytes 65568 | tf_op jit(solution)/shard_map/ppermute | solution.py:20
  57.0 5.5 %collective-permute-done.6 = bf16[128,256]{1,0:T(8,128)(2,1)S(1)} collective-permute-done((bf16[128,256]{1,0:T(8,128)(2,1)S(1)}, bf16[128,256]{1,0:T(8,128)(2,1)S(1)}, u32[]{:S(2)}, u32[]{:S(2)}) %collective-permute-start.6) | collective-permute-done | bytes 65568 | tf_op jit(solution)/shard_map/ppermute | solution.py:20
  62.6 1.7 bitcast_select_fusion
  64.3 55.1 %while.60 = (s32[]{:T(128)}, f32[8,512]{1,0:T(8,128)S(1)}, f32[8,512]{1,0:T(8,128)S(1)}, s32[8]{0:T(128)S(1)}, s32[8]{0:T(128)S(1)}, /*index=5*/bf16[8,512,256]{...) while((s32[]{:T(128)}, f32[8,512]{1,0:T(8,128)S(1)}, ...), condition=%wide.region_7.8_spmd.clone.clone, body=%wide.region_3.7_spmd.clone.sunk.clone | while | flops 135532048 | bytes 2649797 | solution.py:128
  68.8 1.4 fusion.112
  75.6 1.4 fusion.112
  82.5 1.4 fusion.112
  89.4 1.4 fusion.112
  96.3 1.4 fusion.112
  103.2 1.4 fusion.112
  110.1 1.4 fusion.112
  117.0 1.4 fusion.112
  119.4 14.0 %all-gather.1 = f32[64,512]{1,0:T(8,128)S(1)} all-gather(f32[8,512]{1,0:T(8,128)S(1)} %get-tuple-element.259), channel_id=3, replica_groups=mesh['groups'=2,'rows'=4,'mp'=2,'pair'=2] {'rows','pair'}, dimensions={0}, use_global_device_ids=true | all-gather | bytes 147456 | tf_op jit(solution)/shard_map/all_gather | solution.py:26
  133.3 14.0 %all-gather = f32[64,512]{1,0:T(8,128)S(1)} all-gather(f32[8,512]{1,0:T(8,128)S(1)} %get-tuple-element.258), channel_id=2, replica_groups=mesh['groups'=2,'rows'=4,'mp'=2,'pair'=2] {'rows','pair'}, dimensions={0}, use_global_device_ids=true | all-gather | bytes 147456 | tf_op jit(solution)/shard_map/all_gather | solution.py:26
  147.7 61.7 %while.61 = (s32[]{:T(128)}, f32[8,512]{1,0:T(8,128)S(1)}, s32[8]{0:T(128)S(1)}, s32[8]{0:T(128)S(1)}, bf16[8,512,256]{2,1,0:T(8,128)(2,1)}, /*index=5*/bf16[8,5...) while((s32[]{:T(128)}, f32[8,512]{1,0:T(8,128)S(1)}, ...), condition=%wide.region_14.15_spmd.clone.clone, body=%wide.region_10.14_spmd.clone.sunk.clone | while | flops 270534656 | bytes 3170525 | solution.py:145
  152.0 1.4 fusion.115
  159.7 1.4 fusion.115
  167.4 1.4 fusion.115
  175.1 1.4 fusion.115
  182.8 1.4 fusion.115
  190.5 1.4 fusion.115
  198.3 1.4 fusion.115
  206.0 1.4 fusion.115
  209.4 26.1 %psum.7 = f32[8,512]{1,0:T(8,128)S(1)} all-reduce(f32[8,512]{1,0:T(8,128)S(1)} %get-tuple-element.262), channel_id=1, replica_groups=mesh['groups'=2,'rows'=4,'mp'=2,'pair'=2] {'rows','pair'}, use_global_device_ids=true, to_apply=%region_15.16 | all-reduce | flops 4096 | bytes 32768 | tf_op jit(solution)/shard_map/psum | solution.py:146
  235.6 97.7 %while.62 = (s32[]{:T(128)}, f32[8,128,256]{2,1,0:T(8,128)S(1)}, bf16[8,512,256]{2,1,0:T(8,128)(2,1)}, bf16[8,512,256]{2,1,0:T(8,128)(2,1)}, s32[8]{0:T(128)S(1)...) while((s32[]{:T(128)}, f32[8,128,256]{2,1,0:T(8,128)S(1)}, ...), condition=%wide.region_19.20_spmd.clone.clone, body=%wide.region_16.19_spmd.clone.sunk.clone | while | flops 673908224 | bytes 7627025 | solution.py:164
  240.1 1.5 fusion.127
  245.8 2.0 fusion.131
  252.3 1.5 fusion.127
  258.0 2.0 fusion.131
  264.5 1.5 fusion.127
  270.2 2.0 fusion.131
  276.7 1.5 fusion.127
  282.4 2.0 fusion.131
  288.9 1.5 fusion.127
  294.7 2.0 fusion.131
  301.1 1.5 fusion.127
  306.9 2.0 fusion.131
  313.3 1.5 fusion.127
  319.1 2.0 fusion.131
  325.5 1.5 fusion.127
  331.3 2.0 fusion.131
  334.3 30.6 %reduce-scatter.2.cloned.1.call-done = f32[128,256]{1,0:T(8,128)} async-done(((f32[1024,256]{1,0:T(8,128)}), f32[128,256]{1,0:T(8,128)}) %reduce-scatter.2.cloned.1.call-update) | async-done | bytes 131088 | tf_op jit(solution)/shard_map/reduce_scatter | solution.py:167
  364.9 1.5 convert_element_type.21
  (263 shorter events, 126.7 us)
Async XLA Ops:
  7.2 357.7 %reduce-scatter.2.cloned.1.call-start = ((), (), s32[]{:S(2)}) async-start(), calls=%async_computation.1 | async-start | bytes 1179648 | tf_op jit(solution)/shard_map/reduce_scatter | solution.py:167
  7.2 22.3 %collective-permute-start = (bf16[128,256]{1,0:T(8,128)(2,1)}, bf16[128,256]{1,0:T(8,128)(2,1)S(1)}, u32[]{:S(2)}, u32[]{:S(2)}) collective-permute-start(bf16[128,256]{1,0:T(8,128)(2,1)} %param.23), channel_id=1, source_target_pairs={{0,1},{1,4},{4,5},{5,8},{8,9},{9,12},{12,13},{13,0},{2,3},{3,6},{6... | collective-permute-start | bytes 196616 | tf_op jit(solution)/shard_map/ppermute | solution.py:20
  29.5 5.5 %collective-permute-start.1 = (bf16[128,256]{1,0:T(8,128)(2,1)S(1)}, bf16[128,256]{1,0:T(8,128)(2,1)S(1)}, u32[]{:S(2)}, u32[]{:S(2)}) collective-permute-start(bf16[128,256]{1,0:T(8,128)(2,1)S(1)} %collective-permute-done), channel_id=1, source_target_pairs={{0,1},{1,4},{4,5},{5,8},{8,9},{9,12},{12,13},{13,0},{2,3},{3,6},{6... | collective-permute-start | bytes 196616 | tf_op jit(solution)/shard_map/ppermute | solution.py:20
  35.0 5.5 %collective-permute-start.2 = (bf16[128,256]{1,0:T(8,128)(2,1)S(1)}, bf16[128,256]{1,0:T(8,128)(2,1)S(1)}, u32[]{:S(2)}, u32[]{:S(2)}) collective-permute-start(bf16[128,256]{1,0:T(8,128)(2,1)S(1)} %collective-permute-done.1), channel_id=1, source_target_pairs={{0,1},{1,4},{4,5},{5,8},{8,9},{9,12},{12,13},{13,0},{2,3},{3,6},{6... | collective-permute-start | bytes 196616 | tf_op jit(solution)/shard_map/ppermute | solution.py:20
  40.5 5.5 %collective-permute-start.3 = (bf16[128,256]{1,0:T(8,128)(2,1)S(1)}, bf16[128,256]{1,0:T(8,128)(2,1)S(1)}, u32[]{:S(2)}, u32[]{:S(2)}) collective-permute-start(bf16[128,256]{1,0:T(8,128)(2,1)S(1)} %collective-permute-done.2), channel_id=1, source_target_pairs={{0,1},{1,4},{4,5},{5,8},{8,9},{9,12},{12,13},{13,0},{2,3},{3,6},{6... | collective-permute-start | bytes 196616 | tf_op jit(solution)/shard_map/ppermute | solution.py:20
  46.0 5.5 %collective-permute-start.4 = (bf16[128,256]{1,0:T(8,128)(2,1)S(1)}, bf16[128,256]{1,0:T(8,128)(2,1)S(1)}, u32[]{:S(2)}, u32[]{:S(2)}) collective-permute-start(bf16[128,256]{1,0:T(8,128)(2,1)S(1)} %collective-permute-done.3), channel_id=1, source_target_pairs={{0,1},{1,4},{4,5},{5,8},{8,9},{9,12},{12,13},{13,0},{2,3},{3,6},{6... | collective-permute-start | bytes 196616 | tf_op jit(solution)/shard_map/ppermute | solution.py:20
  51.5 5.5 %collective-permute-start.5 = (bf16[128,256]{1,0:T(8,128)(2,1)S(1)}, bf16[128,256]{1,0:T(8,128)(2,1)S(1)}, u32[]{:S(2)}, u32[]{:S(2)}) collective-permute-start(bf16[128,256]{1,0:T(8,128)(2,1)S(1)} %collective-permute-done.4), channel_id=1, source_target_pairs={{0,1},{1,4},{4,5},{5,8},{8,9},{9,12},{12,13},{13,0},{2,3},{3,6},{6... | collective-permute-start | bytes 196616 | tf_op jit(solution)/shard_map/ppermute | solution.py:20
  57.0 5.5 %collective-permute-start.6 = (bf16[128,256]{1,0:T(8,128)(2,1)S(1)}, bf16[128,256]{1,0:T(8,128)(2,1)S(1)}, u32[]{:S(2)}, u32[]{:S(2)}) collective-permute-start(bf16[128,256]{1,0:T(8,128)(2,1)S(1)} %collective-permute-done.5), channel_id=1, source_target_pairs={{0,1},{1,4},{4,5},{5,8},{8,9},{9,12},{12,13},{13,0},{2,3},{3,6},{6... | collective-permute-start | bytes 196616 | tf_op jit(solution)/shard_map/ppermute | solution.py:20
  62.5 1.7 copy-start.1
  147.7 87.9 %copy-start.2 = (s32[3]{0:T(128)S(1)}, s32[3]{0:T(128)}, u32[]{:S(2)}) copy-start(s32[3]{0:T(128)} %constant.247.clone.2) | copy-start | bytes 40
  333.3 1.0 copy-start
Sparse Core Ops, SparseCore 0:
  334.4 30.4 reduce-scatter.1
